TPU v7x, 768 devices: a whole 4x8x12 slice. The times are simulated.
768 devices in a mesh: row: 32 (over z_hi, y), col: 24 (over z_lo, x, core).
Axes of the slice: x: 4, y: 8, z: 12 (z_hi: 4, z_lo: 3; z = z_hi * 3 + z_lo), core: 2. Of those that a mesh axis runs over, the one named last changes fastest.
Arguments:
- start_vectors: float32 [16, 98304], P(None, ('col', 'row')), may hold values from -6 to 6
- tile_values: bfloat16 [32, 24, 8, 128, 128], P('row', 'col'), may hold values from -6 to 6
- tile_scales: float32 [32, 24, 8], P('row', 'col'), may hold values from 0.5 to 2
- tile_rows: int32 [32, 24, 8], P('row', 'col'), may hold values from 0 to 23
- tile_cols: int32 [32, 24, 8], P('row', 'col'), may hold values from 0 to 31
- tile_counts: int32 [32, 24], P('row', 'col'), may hold values from 2 to 8, as said below
Outputs:
- filtered: float32 [16, 98304], P(None, ('col', 'row'))
Inputs may be any that keep to these rules, and one draw needn't show every extreme that they name: `tile_counts`: each device holds between 2 and 8 live tiles; some device holds exactly 8.
All inputs are finite; a program needn't handle non-finite values.
Results may differ from a plain program's by a relative error of at most 0.0037.
Values may be sent and summed in bfloat16 or wider, within the bound.
No kernel may reach another device: no remote copies, remote signals or barrier semaphores. Data moves between devices by JAX's collectives and lax.ppermute only.
A program may use at most 32 MiB of HBM per device.

v0:
```python
import math

import jax
import jax.numpy as jnp
from jax import lax
from jax.sharding import PartitionSpec as P


def contract(blocks, picked, tile_vals, weight, targets, groups, flipped):
    vec_count = blocks.shape[0]
    tile_width = tile_vals.shape[-1]
    shaped = blocks.reshape(vec_count, blocks.shape[1] // tile_width, tile_width)
    chosen = jnp.take(shaped, picked, axis=1)
    if flipped:
        pattern = "vtj,tjk->tvk"
    else:
        pattern = "vtk,tjk->tvj"
    products = jnp.einsum(pattern, chosen, tile_vals, preferred_element_type=jnp.float32)
    products = products * weight[:, None, None]
    onehot = (targets[:, None] == jnp.arange(groups, dtype=jnp.int32)[None, :]).astype(jnp.float32)
    summed = jnp.einsum("tg,tvb->vgb", onehot, products, precision=lax.Precision.HIGH)
    return summed.reshape(vec_count, groups * tile_width)


def body(start_vectors, tile_values, tile_scales, tile_rows, tile_cols, tile_counts):
    tile_vals = tile_values[0, 0]
    row_index = tile_rows[0, 0]
    col_index = tile_cols[0, 0]
    total = tile_vals.shape[0]
    tile_width = tile_vals.shape[-1]
    active = (jnp.arange(total, dtype=jnp.int32) < tile_counts[0, 0]).astype(jnp.float32)
    weight = tile_scales[0, 0] * active
    factor = 0.5 / math.sqrt(2.0 * total * tile_width)
    row_size = lax.axis_size("row")
    col_size = lax.axis_size("col")

    def operate(current):
        rounded = current.astype(jnp.bfloat16)
        row_blocks = lax.all_gather(rounded, "col", axis=1, tiled=True)
        transposed = contract(row_blocks, row_index, tile_vals, weight, col_index, row_size, True)
        col_blocks = lax.all_gather(rounded, "row", axis=1, tiled=True)
        direct = contract(col_blocks, col_index, tile_vals, weight, row_index, col_size, False)
        owned = lax.psum_scatter(direct, "col", scatter_dimension=1, tiled=True) + lax.psum_scatter(
            transposed, "row", scatter_dimension=1, tiled=True
        )
        return factor * owned

    current = operate(start_vectors)
    following = 2.0 * operate(current) - start_vectors
    current = following
    return current


def solution(mesh):
    in_specs = (
        P(None, ("col", "row")),
        P("row", "col", None, None, None),
        P("row", "col", None),
        P("row", "col", None),
        P("row", "col", None),
        P("row", "col"),
    )
    out_specs = P(None, ("col", "row"))
    return jax.shard_map(body, mesh=mesh, in_specs=in_specs, out_specs=out_specs, check_vma=False)
```

profile of v0, /device:TPU:1, one launch (start us, length us, event | category | flops | bytes accessed | tf_op | source)
XLA Modules:
  0.0 914.7 jit_solution(6228329507937142347)
XLA Ops:
  6.5 0.7 compare_select_fusion
  7.9 0.7 convert_element_type.4
  8.6 85.4 %all_gather.12 = bf16[16,4096]{1,0:T(8,128)(2,1)S(1)} all-gather(bf16[16,128]{1,0:T(8,128)(2,1)S(1)} %convert_element_type.4), channel_id=1, replica_groups=mesh['row'=32,'col'=24] {'row'}, dimensions={1}, use_global_device_ids=true | all-gather | bytes 135168 | tf_op jit(solution)/shard_map/all_gather | solution.py:41
  94.1 0.6 copy-done.4
  94.8 0.6 gather_fusion
  95.6 0.7 copy-done.2
  96.6 0.7 copy.42
  97.4 45.3 %all_gather.13 = bf16[16,3072]{1,0:T(8,128)(2,1)S(1)} all-gather(bf16[16,128]{1,0:T(8,128)(2,1)S(1)} %convert_element_type.4), channel_id=1, replica_groups=mesh['row'=32,'col'=24] {'col'}, dimensions={1}, use_global_device_ids=true | all-gather | bytes 102400 | tf_op jit(solution)/shard_map/all_gather | solution.py:39
  142.7 0.6 gather_fusion.1
  143.5 0.3 fusion.8
  143.9 0.9 copy.40
  144.8 60.8 %reduce-scatter.5.cloned.1.call-done = f32[16,128]{1,0:T(8,128)} async-done(((f32[16,3072]{1,0:T(8,128)}), f32[16,128]{1,0:T(8,128)}) %reduce-scatter.5.cloned.1.call-update) | async-done | bytes 8208 | tf_op jit(solution)/shard_map/reduce_scatter | solution.py:43
  205.6 239.3 %reduce-scatter.7.cloned.1.call-done = f32[16,128]{1,0:T(8,128)} async-done(((f32[16,4096]{1,0:T(8,128)}), f32[16,128]{1,0:T(8,128)}) %reduce-scatter.7.cloned.1.call-update) | async-done | bytes 8208 | tf_op jit(solution)/shard_map/reduce_scatter | solution.py:43
  444.9 0.7 multiply_convert_fusion
  445.6 35.5 %all_gather.15 = bf16[16,3072]{1,0:T(8,128)(2,1)S(1)} all-gather(bf16[16,128]{1,0:T(8,128)(2,1)S(1)} %multiply_convert_fusion), channel_id=1, replica_groups=mesh['row'=32,'col'=24] {'col'}, dimensions={1}, use_global_device_ids=true | all-gather | bytes 102400 | tf_op jit(solution)/shard_map/all_gather | solution.py:39
  481.1 72.2 %all_gather.14 = bf16[16,4096]{1,0:T(8,128)(2,1)S(1)} all-gather(bf16[16,128]{1,0:T(8,128)(2,1)S(1)} %multiply_convert_fusion), channel_id=1, replica_groups=mesh['row'=32,'col'=24] {'row'}, dimensions={1}, use_global_device_ids=true | all-gather | bytes 135168 | tf_op jit(solution)/shard_map/all_gather | solution.py:41
  553.4 0.6 gather_fusion.3
  554.0 0.6 gather_fusion.2
  555.2 0.7 copy.41
  556.2 0.3 fusion.4
  556.5 0.9 copy.39
  557.4 110.7 %reduce-scatter.9.cloned.1.call-done = f32[16,128]{1,0:T(8,128)} async-done(((f32[16,3072]{1,0:T(8,128)}), f32[16,128]{1,0:T(8,128)}) %reduce-scatter.9.cloned.1.call-update) | async-done | bytes 8208 | tf_op jit(solution)/shard_map/reduce_scatter | solution.py:43
  668.1 238.8 %reduce-scatter.11.cloned.1.call-done = f32[16,128]{1,0:T(8,128)} async-done(((f32[16,4096]{1,0:T(8,128)}), f32[16,128]{1,0:T(8,128)}) %reduce-scatter.11.cloned.1.call-update) | async-done | bytes 8208 | tf_op jit(solution)/shard_map/reduce_scatter | solution.py:43
  906.8 1.3 multiply_subtract_fusion
  (32 shorter events, 2.0 us)
Async XLA Ops:
  6.5 88.8 %copy-start = (bf16[1,1,8,128,128]{4,3,2,1,0:T(8,128)(2,1)S(1)}, bf16[1,1,8,128,128]{4,3,2,1,0:T(8,128)(2,1)}, u32[]{:S(2)}) copy-start(bf16[1,1,8,128,128]{4,3,2,1,0:T(8,128)(2,1)} %param.11) | copy-start | bytes 786436
  6.5 0.7 copy-start.3
  6.5 199.0 %reduce-scatter.5.cloned.1.call-start = ((), (), s32[]{:S(2)}) async-start(), calls=%async_computation.4 | async-start | bytes 204800 | tf_op jit(solution)/shard_map/reduce_scatter | solution.py:43
  94.1 0.7 copy-start.4
  95.6 0.7 copy-start.2
  97.3 347.5 %reduce-scatter.7.cloned.1.call-start = ((), (), s32[]{:S(2)}) async-start(), calls=%async_computation.5 | async-start | bytes 270336 | tf_op jit(solution)/shard_map/reduce_scatter | solution.py:43
  144.8 523.3 %reduce-scatter.9.cloned.1.call-start = ((), (), s32[]{:S(2)}) async-start(), calls=%async_computation.6 | async-start | bytes 204800 | tf_op jit(solution)/shard_map/reduce_scatter | solution.py:43
  555.9 350.9 %reduce-scatter.11.cloned.1.call-start = ((), (), s32[]{:S(2)}) async-start(), calls=%async_computation.7 | async-start | bytes 270336 | tf_op jit(solution)/shard_map/reduce_scatter | solution.py:43
  557.4 349.4 %copy-start.1 = (f32[16,128]{1,0:T(8,128)S(1)}, f32[16,128]{1,0:T(8,128)}, u32[]{:S(2)}) copy-start(f32[16,128]{1,0:T(8,128)} %param.10) | copy-start | bytes 24580
Sparse Core Ops, SparseCore 0:
  97.5 108.0 reduce-scatter.4
  210.4 234.4 reduce-scatter.6
  556.0 112.0 reduce-scatter.8
  672.7 234.0 reduce-scatter.10
where the time goes:
time: 919 us; the launch traced here: 915 us
  waiting for transfers between devices  650 us (71%)
  blocking collectives  239 us (26%)
  between operations  13.9 us (2%)
    reduce_scatter x2, waiting for transfers between devices, operate(): lax.psum_scatter(transposed, 'row', scatter_dimension=1, tiled=True)  478 us
    reduce_scatter x2, waiting for transfers between devices, operate(): lax.psum_scatter(direct, 'col', scatter_dimension=1, tiled=True)  171 us
    all_gather x2, blocking collectives, operate(): col_blocks = lax.all_gather(rounded, 'row', axis=1, tiled=True)  158 us
    all_gather x2, blocking collectives, operate(): row_blocks = lax.all_gather(rounded, 'col', axis=1, tiled=True)  80.8 us
  transfers between devices with their start and end apart: 4, of which 4 were waited for; matrix products, arithmetic and copies ran while one was open for 0% of the time, Pallas kernels for 0%

commit v1 on v0

v1 whole, which is shorter than its diff:
```python
import functools
import math

import jax
import jax.numpy as jnp
from jax import lax
from jax.experimental import pallas as pl
from jax.experimental.pallas import tpu as pltpu
from jax.sharding import PartitionSpec as P


def product_kernel(flipped, count_ref, scale_ref, from_ref, to_ref, blocks_ref, tiles_ref, out_ref, acc_ref):
    acc_ref[...] = jnp.zeros_like(acc_ref)
    for slot in range(tiles_ref.shape[0]):
        weight = jnp.where(slot < count_ref[0], scale_ref[slot], 0.0)
        contracted = 0 if flipped else 1
        product = lax.dot_general(
            blocks_ref[from_ref[slot]],
            tiles_ref[slot],
            (((1,), (contracted,)), ((), ())),
            preferred_element_type=jnp.float32,
        )
        target = to_ref[slot]
        acc_ref[target] = acc_ref[target] + product * weight
    out_ref[...] = acc_ref[...].astype(out_ref.dtype)


def products(blocks, tile_vals, count, scales, source, target, groups, flipped):
    vec_count, width = blocks.shape[1:]
    smem = pl.BlockSpec(memory_space=pltpu.SMEM)
    vmem = pl.BlockSpec(memory_space=pltpu.VMEM)
    slots = tile_vals.shape[0]
    return pl.pallas_call(
        functools.partial(product_kernel, flipped),
        out_shape=jax.ShapeDtypeStruct((groups, vec_count, width), jnp.bfloat16),
        in_specs=[smem, smem, smem, smem, vmem, vmem],
        out_specs=vmem,
        scratch_shapes=[pltpu.VMEM((groups, vec_count, width), jnp.float32)],
        cost_estimate=pl.CostEstimate(
            flops=2 * slots * vec_count * width * width, bytes_accessed=2 * tile_vals.size, transcendentals=0
        ),
        name="flipped" if flipped else "direct",
    )(count, scales, source, target, blocks, tile_vals)


def body(start_vectors, tile_values, tile_scales, tile_rows, tile_cols, tile_counts):
    tile_vals = tile_values[0, 0]
    scales = tile_scales[0, 0]
    row_index = tile_rows[0, 0]
    col_index = tile_cols[0, 0]
    count = tile_counts[0]
    total, tile_width = tile_vals.shape[:2]
    factor = 0.5 / math.sqrt(2.0 * total * tile_width)
    row_size = lax.axis_size("row")
    col_size = lax.axis_size("col")

    def everywhere(block, size):
        return jnp.broadcast_to(block[None], (size, *block.shape))

    def exchange(blocks, axis):
        return lax.all_to_all(blocks, axis, 0, 0, tiled=True)

    def operate(current):
        rounded = current.astype(jnp.bfloat16)
        row_blocks = exchange(everywhere(rounded, col_size), "col")
        transposed = products(row_blocks, tile_vals, count, scales, row_index, col_index, row_size, True)
        col_blocks = exchange(everywhere(rounded, row_size), "row")
        direct = products(col_blocks, tile_vals, count, scales, col_index, row_index, col_size, False)
        from_col = jnp.sum(exchange(direct, "col"), axis=0, dtype=jnp.float32)
        from_row = jnp.sum(exchange(transposed, "row"), axis=0, dtype=jnp.float32)
        return factor * (from_col + from_row)

    following = operate(start_vectors)
    return 2.0 * operate(following) - start_vectors


def solution(mesh):
    in_specs = (
        P(None, ("col", "row")),
        P("row", "col", None, None, None),
        P("row", "col", None),
        P("row", "col", None),
        P("row", "col", None),
        P("row", "col"),
    )
    out_specs = P(None, ("col", "row"))
    return jax.shard_map(body, mesh=mesh, in_specs=in_specs, out_specs=out_specs, check_vma=False)
```

time: 919 us -> 150 us (0.16)
  waiting for transfers between devices: 650 us -> 61.6 us
  blocking collectives: 239 us -> 32.2 us
  starting transfers between devices: 0.13 us -> 44 us
  between operations: 13.9 us -> 0.77 us
    reduce_scatter x4 -> x0, waiting for transfers between devices: 649 us -> none  [the longest x2 478 us: operate(): lax.psum_scatter(transposed, 'row', scatter_dimension=1, tiled=True)]
    all_gather x4 -> x0, blocking collectives: 239 us -> none  [the longest x2 158 us: operate(): col_blocks = lax.all_gather(rounded, 'row', axis=1, tiled=True)]
    all_to_all x0 -> x6, waiting for transfers between devices: none -> 61.6 us  [exchange(): return lax.all_to_all(blocks, axis, 0, 0, tiled=True)]
    all_to_all x0 -> x6, starting transfers between devices: none -> 44 us  [exchange(): return lax.all_to_all(blocks, axis, 0, 0, tiled=True)]
    all_to_all x0 -> x2, blocking collectives: none -> 32.2 us  [exchange(): return lax.all_to_all(blocks, axis, 0, 0, tiled=True)]
  transfers between devices with their start and end apart: 4 -> 6, of which waited for: 4 -> 6; matrix products, arithmetic and copies ran while one was open for 0% -> 0% of each run, Pallas kernels for 0% -> 5%
where the time goes in v1:
time: 150 us
  waiting for transfers between devices  61.6 us (41%)
  starting transfers between devices  44 us (29%)
  blocking collectives  32.2 us (21%)
  Pallas kernels  7.6 us (5%)
  local copies, waits for them, and re-layouts  1.98 us (1%)
    all_to_all x6, waiting for transfers between devices, exchange(): return lax.all_to_all(blocks, axis, 0, 0, tiled=True)  61.6 us
    all_to_all x6, starting transfers between devices, exchange(): return lax.all_to_all(blocks, axis, 0, 0, tiled=True)  44 us
    all_to_all x2, blocking collectives, exchange(): return lax.all_to_all(blocks, axis, 0, 0, tiled=True)  32.2 us
    pallas_call x4, Pallas kernels, products(): pl.pallas_call(functools.partial(product_kernel, flipped), out_shape=jax....  7.6 us
  transfers between devices with their start and end apart: 6, of which 6 were waited for; matrix products, arithmetic and copies ran while one was open for 0% of the time, Pallas kernels for 5%

profile of v1, /device:TPU:1, one launch (start us, length us, event | category | flops | bytes accessed | tf_op | source)
XLA Modules:
  0.0 149.6 jit_solution(11754245122327877821)
XLA Ops:
  0.0 0.7 convert_element_type.22
  0.7 21.1 %all_to_all.40.blocks_ref = bf16[24,16,128]{2,1,0:T(8,128)(2,1)} all-to-all(bf16[24,16,128]{2,1,0:T(8,128)(2,1)S(1)} %broadcast_in_dim.9), channel_id=1, replica_groups=mesh['row'=32,'col'=24] {'col'}, dimensions={0} | all-to-all | bytes 196608 | tf_op jit(solution)/shard_map/all_to_all | solution.py:61
  21.8 0.7 broadcast_in_dim.8
  22.5 15.3 %all-to-all-start = ((bf16[32,16,128]{2,1,0:T(8,128)(2,1)}), bf16[32,16,128]{2,1,0:T(8,128)(2,1)S(1)}, u32[]{:S(2)}, u32[]{:S(2)}) async-start(bf16[32,16,128]{2,1,0:T(8,128)(2,1)} %broadcast_in_dim.8), calls=%async_computation | async-start | bytes 262144 | tf_op jit(solution)/shard_map/all_to_all | solution.py:61
  38.5 1.9 %flipped.2 = bf16[32,16,128]{2,1,0:T(8,128)(2,1)} custom-call(s32[1]{0:T(128)} %bitcast.6.count_ref, f32[8]{0:T(128)} %bitcast.13, s32[8]{0:T(128)} %bitcast.21, s32[8]{0:T(128)} %bitcast.17, bf16[24,16,128]{2,1,0:T(8,128)(2,1)} %all_to_all.40.blocks_ref, bf16[8,128,128]{2,1,0:T(8,128)(2,1)} %bitcast.9), custom_call_target="tpu_custom_call" | custom-call | flops 4194304 | bytes 262144 | tf_op jit(solution)/shard_map/flipped/pallas_call | solution.py:33
  40.3 11.4 %all-to-all-done.blocks_ref = bf16[32,16,128]{2,1,0:T(8,128)(2,1)S(1)} async-done(((bf16[32,16,128]{2,1,0:T(8,128)(2,1)}), bf16[32,16,128]{2,1,0:T(8,128)(2,1)S(1)}, u32[]{:S(2)}, u32[]{:S(2)}) %all-to-all-start) | async-done | bytes 131104 | tf_op jit(solution)/shard_map/all_to_all | solution.py:61
  51.7 5.1 %all-to-all-start.3 = ((bf16[32,16,128]{2,1,0:T(8,128)(2,1)}), bf16[32,16,128]{2,1,0:T(8,128)(2,1)S(1)}, u32[]{:S(2)}, u32[]{:S(2)}) async-start(bf16[32,16,128]{2,1,0:T(8,128)(2,1)} %flipped.2), calls=%async_computation.3 | async-start | bytes 262144 | tf_op jit(solution)/shard_map/all_to_all | solution.py:61
  56.8 1.9 %direct.2 = bf16[24,16,128]{2,1,0:T(8,128)(2,1)} custom-call(s32[1]{0:T(128)} %bitcast.5.count_ref, f32[8]{0:T(128)} %bitcast.14, s32[8]{0:T(128)} %bitcast.18, s32[8]{0:T(128)} %bitcast.22, bf16[32,16,128]{2,1,0:T(8,128)(2,1)} %copy-done, bf16[8,128,128]{2,1,0:T(8,128)(2,1)} %bitcast.10), custom_call_target="tpu_custom_call" | custom-call | flops 4194304 | bytes 262144 | tf_op jit(solution)/shard_map/direct/pallas_call | solution.py:33
  58.8 11.9 %all-to-all-done.3 = bf16[32,16,128]{2,1,0:T(8,128)(2,1)S(1)} async-done(((bf16[32,16,128]{2,1,0:T(8,128)(2,1)}), bf16[32,16,128]{2,1,0:T(8,128)(2,1)S(1)}, u32[]{:S(2)}, u32[]{:S(2)}) %all-to-all-start.3) | async-done | bytes 131104 | tf_op jit(solution)/shard_map/all_to_all | solution.py:61
  70.7 5.7 %all-to-all-start.1 = ((bf16[24,16,128]{2,1,0:T(8,128)(2,1)}), bf16[24,16,128]{2,1,0:T(8,128)(2,1)S(1)}, u32[]{:S(2)}, u32[]{:S(2)}) async-start(bf16[24,16,128]{2,1,0:T(8,128)(2,1)} %direct.2), calls=%async_computation.1 | async-start | bytes 196608 | tf_op jit(solution)/shard_map/all_to_all | solution.py:61
  76.4 7.2 %all-to-all-done.1 = bf16[24,16,128]{2,1,0:T(8,128)(2,1)S(1)} async-done(((bf16[24,16,128]{2,1,0:T(8,128)(2,1)}), bf16[24,16,128]{2,1,0:T(8,128)(2,1)S(1)}, u32[]{:S(2)}, u32[]{:S(2)}) %all-to-all-start.1) | async-done | bytes 98336 | tf_op jit(solution)/shard_map/all_to_all | solution.py:61
  83.8 11.0 %all_to_all.41.blocks_ref = bf16[24,16,128]{2,1,0:T(8,128)(2,1)} all-to-all(bf16[24,16,128]{2,1,0:T(8,128)(2,1)S(1)} %broadcast_in_dim.11), channel_id=1, replica_groups=mesh['row'=32,'col'=24] {'col'}, dimensions={0} | all-to-all | bytes 196608 | tf_op jit(solution)/shard_map/all_to_all | solution.py:61
  94.8 0.7 broadcast_in_dim.10
  95.4 6.9 %all-to-all-start.4 = ((bf16[32,16,128]{2,1,0:T(8,128)(2,1)}), bf16[32,16,128]{2,1,0:T(8,128)(2,1)S(1)}, u32[]{:S(2)}, u32[]{:S(2)}) async-start(bf16[32,16,128]{2,1,0:T(8,128)(2,1)} %broadcast_in_dim.10), calls=%async_computation.4 | async-start | bytes 262144 | tf_op jit(solution)/shard_map/all_to_all | solution.py:61
  102.4 1.9 %flipped.3 = bf16[32,16,128]{2,1,0:T(8,128)(2,1)} custom-call(s32[1]{0:T(128)} %bitcast.8.count_ref, f32[8]{0:T(128)} %bitcast.15, s32[8]{0:T(128)} %bitcast.23, s32[8]{0:T(128)} %bitcast.19, bf16[24,16,128]{2,1,0:T(8,128)(2,1)} %all_to_all.41.blocks_ref, bf16[8,128,128]{2,1,0:T(8,128)(2,1)} %bitcast.11), custom_call_target="tpu_custom_call" | custom-call | flops 4194304 | bytes 262144 | tf_op jit(solution)/shard_map/flipped/pallas_call | solution.py:33
  104.2 12.0 %all-to-all-done.4.blocks_ref = bf16[32,16,128]{2,1,0:T(8,128)(2,1)S(1)} async-done(((bf16[32,16,128]{2,1,0:T(8,128)(2,1)}), bf16[32,16,128]{2,1,0:T(8,128)(2,1)S(1)}, u32[]{:S(2)}, u32[]{:S(2)}) %all-to-all-start.4) | async-done | bytes 131104 | tf_op jit(solution)/shard_map/all_to_all | solution.py:61
  116.2 0.6 copy-done.1
  116.9 5.3 %all-to-all-start.7 = ((bf16[32,16,128]{2,1,0:T(8,128)(2,1)}), bf16[32,16,128]{2,1,0:T(8,128)(2,1)S(1)}, u32[]{:S(2)}, u32[]{:S(2)}) async-start(bf16[32,16,128]{2,1,0:T(8,128)(2,1)} %flipped.3), calls=%async_computation.7 | async-start | bytes 262144 | tf_op jit(solution)/shard_map/all_to_all | solution.py:61
  122.2 1.9 %direct.3 = bf16[24,16,128]{2,1,0:T(8,128)(2,1)} custom-call(s32[1]{0:T(128)} %bitcast.7.count_ref, f32[8]{0:T(128)} %bitcast.16, s32[8]{0:T(128)} %bitcast.20, s32[8]{0:T(128)} %bitcast.24, bf16[32,16,128]{2,1,0:T(8,128)(2,1)} %copy-done.1, bf16[8,128,128]{2,1,0:T(8,128)(2,1)} %bitcast.12), custom_call_target="tpu_custom_call" | custom-call | flops 4194304 | bytes 262144 | tf_op jit(solution)/shard_map/direct/pallas_call | solution.py:33
  124.1 11.9 %all-to-all-done.7 = bf16[32,16,128]{2,1,0:T(8,128)(2,1)S(1)} async-done(((bf16[32,16,128]{2,1,0:T(8,128)(2,1)}), bf16[32,16,128]{2,1,0:T(8,128)(2,1)S(1)}, u32[]{:S(2)}, u32[]{:S(2)}) %all-to-all-start.7) | async-done | bytes 131104 | tf_op jit(solution)/shard_map/all_to_all | solution.py:61
  136.0 5.6 %all-to-all-start.5 = ((bf16[24,16,128]{2,1,0:T(8,128)(2,1)}), bf16[24,16,128]{2,1,0:T(8,128)(2,1)S(1)}, u32[]{:S(2)}, u32[]{:S(2)}) async-start(bf16[24,16,128]{2,1,0:T(8,128)(2,1)} %direct.3), calls=%async_computation.5 | async-start | bytes 196608 | tf_op jit(solution)/shard_map/all_to_all | solution.py:61
  141.7 0.0 copy-start.2
  141.7 7.2 %all-to-all-done.5 = bf16[24,16,128]{2,1,0:T(8,128)(2,1)S(1)} async-done(((bf16[24,16,128]{2,1,0:T(8,128)(2,1)}), bf16[24,16,128]{2,1,0:T(8,128)(2,1)S(1)}, u32[]{:S(2)}, u32[]{:S(2)}) %all-to-all-start.5) | async-done | bytes 98336 | tf_op jit(solution)/shard_map/all_to_all | solution.py:61
  149.0 0.6 multiply_subtract_fusion
  (11 shorter events, 0.2 us)
Async XLA Ops:
  22.5 29.2 %all-to-all-start = ((bf16[32,16,128]{2,1,0:T(8,128)(2,1)}), bf16[32,16,128]{2,1,0:T(8,128)(2,1)S(1)}, u32[]{:S(2)}, u32[]{:S(2)}) async-start(bf16[32,16,128]{2,1,0:T(8,128)(2,1)} %broadcast_in_dim.8), calls=%async_computation | async-start | bytes 262144 | tf_op jit(solution)/shard_map/all_to_all | solution.py:61
  51.7 5.1 %copy-start = (bf16[32,16,128]{2,1,0:T(8,128)(2,1)}, bf16[32,16,128]{2,1,0:T(8,128)(2,1)S(1)}, u32[]{:S(2)}) copy-start(bf16[32,16,128]{2,1,0:T(8,128)(2,1)S(1)} %all-to-all-done.blocks_ref) | copy-start | bytes 393220
  51.7 19.0 %all-to-all-start.3 = ((bf16[32,16,128]{2,1,0:T(8,128)(2,1)}), bf16[32,16,128]{2,1,0:T(8,128)(2,1)S(1)}, u32[]{:S(2)}, u32[]{:S(2)}) async-start(bf16[32,16,128]{2,1,0:T(8,128)(2,1)} %flipped.2), calls=%async_computation.3 | async-start | bytes 262144 | tf_op jit(solution)/shard_map/all_to_all | solution.py:61
  70.7 13.0 %all-to-all-start.1 = ((bf16[24,16,128]{2,1,0:T(8,128)(2,1)}), bf16[24,16,128]{2,1,0:T(8,128)(2,1)S(1)}, u32[]{:S(2)}, u32[]{:S(2)}) async-start(bf16[24,16,128]{2,1,0:T(8,128)(2,1)} %direct.2), calls=%async_computation.1 | async-start | bytes 196608 | tf_op jit(solution)/shard_map/all_to_all | solution.py:61
  95.4 20.8 %all-to-all-start.4 = ((bf16[32,16,128]{2,1,0:T(8,128)(2,1)}), bf16[32,16,128]{2,1,0:T(8,128)(2,1)S(1)}, u32[]{:S(2)}, u32[]{:S(2)}) async-start(bf16[32,16,128]{2,1,0:T(8,128)(2,1)} %broadcast_in_dim.10), calls=%async_computation.4 | async-start | bytes 262144 | tf_op jit(solution)/shard_map/all_to_all | solution.py:61
  116.2 0.6 copy-start.1
  116.9 19.1 %all-to-all-start.7 = ((bf16[32,16,128]{2,1,0:T(8,128)(2,1)}), bf16[32,16,128]{2,1,0:T(8,128)(2,1)S(1)}, u32[]{:S(2)}, u32[]{:S(2)}) async-start(bf16[32,16,128]{2,1,0:T(8,128)(2,1)} %flipped.3), calls=%async_computation.7 | async-start | bytes 262144 | tf_op jit(solution)/shard_map/all_to_all | solution.py:61
  136.0 12.9 %all-to-all-start.5 = ((bf16[24,16,128]{2,1,0:T(8,128)(2,1)}), bf16[24,16,128]{2,1,0:T(8,128)(2,1)S(1)}, u32[]{:S(2)}, u32[]{:S(2)}) async-start(bf16[24,16,128]{2,1,0:T(8,128)(2,1)} %direct.3), calls=%async_computation.5 | async-start | bytes 196608 | tf_op jit(solution)/shard_map/all_to_all | solution.py:61
  141.7 7.3 %copy-start.2 = (f32[16,128]{1,0:T(8,128)S(1)}, f32[16,128]{1,0:T(8,128)}, u32[]{:S(2)}) copy-start(f32[16,128]{1,0:T(8,128)} %param.6) | copy-start | bytes 24580

commit v2 on v1

v2 whole, which is shorter than its diff:
```python
import functools
import math

import jax
import jax.numpy as jnp
from jax import lax
from jax.experimental import pallas as pl
from jax.experimental.pallas import tpu as pltpu
from jax.sharding import Mesh
from jax.sharding import PartitionSpec as P


def product_kernel(flipped, count_ref, scale_ref, row_ref, col_ref, blocks_ref, tiles_ref, out_ref, acc_ref):
    acc_ref[...] = jnp.zeros_like(acc_ref)
    cores, slots = tiles_ref.shape[:2]
    for core in range(cores):
        for slot in range(slots):
            weight = jnp.where(slot < count_ref[core], scale_ref[core, slot], 0.0)
            row = row_ref[core, slot]
            col = col_ref[core, slot] * cores + core
            source, target, contracted = (row, col, 0) if flipped else (col, row, 1)
            product = lax.dot_general(
                blocks_ref[source],
                tiles_ref[core, slot],
                (((1,), (contracted,)), ((), ())),
                preferred_element_type=jnp.float32,
            )
            acc_ref[target] = acc_ref[target] + product * weight
    out_ref[...] = acc_ref[...].astype(out_ref.dtype)


def products(blocks, tile_vals, count, scales, rows, cols, groups, flipped):
    vec_count, width = blocks.shape[1:]
    smem = pl.BlockSpec(memory_space=pltpu.SMEM)
    vmem = pl.BlockSpec(memory_space=pltpu.VMEM)
    return pl.pallas_call(
        functools.partial(product_kernel, flipped),
        out_shape=jax.ShapeDtypeStruct((groups, vec_count, width), jnp.bfloat16),
        in_specs=[smem, smem, smem, smem, vmem, vmem],
        out_specs=vmem,
        scratch_shapes=[pltpu.VMEM((groups, vec_count, width), jnp.float32)],
        cost_estimate=pl.CostEstimate(
            flops=2 * vec_count * tile_vals.size, bytes_accessed=2 * tile_vals.size, transcendentals=0
        ),
        name="flipped" if flipped else "direct",
    )(count, scales, rows, cols, blocks, tile_vals)


def body(start_vectors, tile_values, tile_scales, tile_rows, tile_cols, tile_counts):
    total, tile_width = tile_values.shape[2:4]
    vec_count = start_vectors.shape[0]
    factor = 0.5 / math.sqrt(2.0 * total * tile_width)
    row_size = lax.axis_size("row")
    pair_size = lax.axis_size("pair")
    core_size = lax.axis_size("core")
    core = lax.axis_index("core")

    def both_cores(array):
        return lax.all_gather(array, "core", axis=0, tiled=True)

    tile_vals = both_cores(tile_values[0])
    scales = both_cores(tile_scales[0])
    rows = both_cores(tile_rows[0])
    cols = both_cores(tile_cols[0])
    count = both_cores(tile_counts[0])

    def exchange(blocks, axis):
        return lax.all_to_all(blocks, axis, 0, 0, tiled=True)

    def fetch(blocks, axis, size):
        got = exchange(jnp.broadcast_to(blocks[None], (size, *blocks.shape)), axis)
        return got.reshape(size * core_size, vec_count, tile_width)

    def give(partial, axis, size):
        got = exchange(partial.reshape(size, core_size, vec_count, tile_width), axis)
        return jnp.sum(got, axis=0, dtype=jnp.float32)

    def flipped_chain(blocks):
        row_blocks = fetch(blocks, "pair", pair_size)
        partial = products(row_blocks, tile_vals, count, scales, rows, cols, row_size * core_size, True)
        return give(partial, "row", row_size)

    def direct_chain(blocks):
        col_blocks = fetch(blocks, "row", row_size)
        partial = products(col_blocks, tile_vals, count, scales, rows, cols, pair_size * core_size, False)
        return give(partial, "pair", pair_size)

    def operate(blocks):
        mine = lax.cond(core == 0, flipped_chain, direct_chain, blocks)
        return factor * jnp.sum(both_cores(mine[None]), axis=0)

    following = operate(both_cores(start_vectors.astype(jnp.bfloat16)[None]))
    last = operate(following.astype(jnp.bfloat16))
    return 2.0 * lax.dynamic_index_in_dim(last, core, 0, keepdims=False) - start_vectors


def solution(mesh):
    rows, cols = mesh.devices.shape
    split = Mesh(mesh.devices.reshape(rows, cols // 2, 2), ("row", "pair", "core"))
    columns = ("pair", "core")
    in_specs = (
        P(None, (*columns, "row")),
        P("row", columns, None, None, None),
        P("row", columns, None),
        P("row", columns, None),
        P("row", columns, None),
        P("row", columns),
    )
    out_specs = P(None, (*columns, "row"))
    return jax.shard_map(body, mesh=split, in_specs=in_specs, out_specs=out_specs, check_vma=False)
```

time: 150 us -> 109 us (0.73)
  blocking collectives: 32.2 us -> 101 us
  waiting for transfers between devices: 61.6 us -> 0 us
  starting transfers between devices: 44 us -> 0 us
  Pallas kernels: 7.6 us -> 4.01 us
    all_to_all x6 -> x0, waiting for transfers between devices: 61.6 us -> none  [exchange(): return lax.all_to_all(blocks, axis, 0, 0, tiled=True)]
    all_to_all x6 -> x0, starting transfers between devices: 44 us -> none  [exchange(): return lax.all_to_all(blocks, axis, 0, 0, tiled=True)]
    all_to_all x2 -> x4, blocking collectives: 32.2 us -> 67.6 us  [exchange(): return lax.all_to_all(blocks, axis, 0, 0, tiled=True)]
    all_gather x0 -> x8, blocking collectives: none -> 33 us  [both_cores(): return lax.all_gather(array, 'core', axis=0, tiled=True)]
    pallas_call x4 -> x2, Pallas kernels: 7.6 us -> 4.01 us  [products(): pl.pallas_call(functools.partial(product_kernel, flipped), out_shape=jax....]
    unnamed x6 -> x11, local copies, waits for them, and re-layouts: 0.65 us -> 2.77 us
  transfers between devices with their start and end apart: 6 -> 0, of which waited for: 6 -> 0; matrix products, arithmetic and copies ran while one was open for 0% -> 0% of each run, Pallas kernels for 5% -> 0%
where the time goes in v2:
time: 109 us
  blocking collectives  101 us (93%)
  Pallas kernels  4.01 us (4%)
  local copies, waits for them, and re-layouts  2.84 us (3%)
    all_to_all x4, blocking collectives, exchange(): return lax.all_to_all(blocks, axis, 0, 0, tiled=True)  67.6 us
    all_gather x8, blocking collectives, both_cores(): return lax.all_gather(array, 'core', axis=0, tiled=True)  33 us
    pallas_call x2, Pallas kernels, products(): pl.pallas_call(functools.partial(product_kernel, flipped), out_shape=jax....  4.01 us
    unnamed x11, local copies, waits for them, and re-layouts  2.77 us

profile of v2, /device:TPU:1, one launch (start us, length us, event | category | flops | bytes accessed | tf_op | source)
XLA Modules:
  0.0 108.8 jit_solution(12732819456174288865)
XLA Ops:
  0.7 1.4 %dynamic-slice = u32[1]{0:T(128)} dynamic-slice(u32[768]{0:T(1024)} %constant.33, u32[]{:T(128)S(6)} %add.5), dynamic_slice_sizes={1} | dynamic-slice | bytes 12
  2.0 0.0 copy-start.1
  2.0 0.8 bitcast_dynamic-update-slice_fusion
  2.8 12.0 %all-reduce = s32[2]{0:T(128)S(1)} all-reduce(s32[2]{0:T(128)S(1)} %bitcast_dynamic-update-slice_fusion), channel_id=3, replica_groups=mesh['row'=32,'pair'=12,'core'=2] {'core'}, use_global_device_ids=true, to_apply=%add | all-reduce | flops 2 | bytes 16 | tf_op jit(solution)/shard_map/all_gather | solution.py:59
  14.8 0.0 copy-done.1
  14.8 1.8 %all-gather.2 = f32[2,1,8]{2,1,0:T(1,128)S(1)} all-gather(f32[1,1,8]{2,1,0:T(1,128)S(1)} %copy-done.1), channel_id=4, replica_groups=mesh['row'=32,'pair'=12,'core'=2] {'core'}, dimensions={0}, use_global_device_ids=true | all-gather | bytes 96 | tf_op jit(solution)/shard_map/all_gather | solution.py:59
  16.5 0.0 copy-done.2
  16.6 1.8 %all-gather.3 = s32[2,1,8]{2,1,0:T(1,128)S(1)} all-gather(s32[1,1,8]{2,1,0:T(1,128)S(1)} %copy-done.2), channel_id=5, replica_groups=mesh['row'=32,'pair'=12,'core'=2] {'core'}, dimensions={0}, use_global_device_ids=true | all-gather | bytes 96 | tf_op jit(solution)/shard_map/all_gather | solution.py:59
  18.4 0.7 copy-done.3
  19.0 1.8 %all-gather.4 = s32[2,1,8]{2,1,0:T(1,128)S(1)} all-gather(s32[1,1,8]{2,1,0:T(1,128)S(1)} %copy-done.3), channel_id=6, replica_groups=mesh['row'=32,'pair'=12,'core'=2] {'core'}, dimensions={0}, use_global_device_ids=true | all-gather | bytes 96 | tf_op jit(solution)/shard_map/all_gather | solution.py:59
  20.8 0.0 copy-done
  20.8 1.8 %all-gather = bf16[32,128]{1,0:T(8,128)(2,1)S(1)} all-gather(bf16[16,128]{1,0:T(8,128)(2,1)S(1)} %convert_element_type.23), channel_id=2, replica_groups=mesh['row'=32,'pair'=12,'core'=2] {'core'}, dimensions={0}, use_global_device_ids=true | all-gather | bytes 12288 | tf_op jit(solution)/shard_map/all_gather | solution.py:59
  22.6 2.4 %all-gather.5 = bf16[2,1,8,128,128]{4,3,2,1,0:T(8,128)(2,1)S(1)} all-gather(bf16[1,1,8,128,128]{4,3,2,1,0:T(8,128)(2,1)} %param.11), channel_id=7, replica_groups=mesh['row'=32,'pair'=12,'core'=2] {'core'}, dimensions={0}, use_global_device_ids=true | all-gather | bytes 786432 | tf_op jit(solution)/shard_map/all_gather | solution.py:59
  25.0 39.7 %conditional.2 = (f32[2,16,128]{2,1,0:T(8,128)S(1)}) conditional(s32[]{:T(128)} %convert_element_type.22, (bf16[2,16,128]{2,1,0:T(8,128)(2,1)S(1)}, s32[2]{0:T(128)S(1)}, f32[2,8]{1,0:T(2,128)S(1)}, s32[2,8]{1,0:T(2,128)S(1)}, s32[2,8]{1,0:T(2,128)S(1)}, /*index=5*/bf16[2,8,128,128]{3,2,1,0:T(8,128)(2,1)S(1)}) %tuple.37, ...), branch_computations={%region_0.0_spmd, %region_2.0_spmd} | conditional | flops 8646656 | bytes 1630216 | solution.py:89
  25.0 25.1 %all_to_all.32 = bf16[32,2,16,128]{3,2,1,0:T(8,128)(2,1)} all-to-all(bf16[32,2,16,128]{3,2,1,0:T(8,128)(2,1)S(1)} %broadcast_in_dim.3), channel_id=1, replica_groups=mesh['row'=32,'pair'=12,'core'=2] {'row'}, dimensions={0} | all-to-all | bytes 524288 | tf_op jit(solution)/shard_map/cond/branch_0_fun/all_to_all | solution.py:68
  50.1 2.0 %direct.2 = bf16[24,16,128]{2,1,0:T(8,128)(2,1)} custom-call(s32[2]{0:T(128)S(1)} %get-tuple-element.58.count_ref, f32[2,8]{1,0:T(2,128)S(1)} %get-tuple-element.60.scale_ref, s32[2,8]{1,0:T(2,128)S(1)} %get-tuple-element.61.row_ref, s32[2,8]{1,0:T(2,128)S(1)} %get-tuple-element.62.col_ref, bf16[64,16,128]{2,1,0:T(8,128)(2,1)} %bitcast.26, ...), custom_call_target="tpu_custom_call" | custom-call | flops 8388608 | bytes 524288 | tf_op jit(solution)/shard_map/cond/branch_0_fun/direct/pallas_call | solution.py:36
  52.1 12.5 %all_to_all.33 = bf16[12,2,16,128]{3,2,1,0:T(8,128)(2,1)S(1)} all-to-all(bf16[12,2,16,128]{3,2,1,0:T(8,128)(2,1)} %bitcast.30), channel_id=1, replica_groups=mesh['row'=32,'pair'=12,'core'=2] {'pair'}, dimensions={0} | all-to-all | bytes 196608 | tf_op jit(solution)/shard_map/cond/branch_0_fun/all_to_all | solution.py:68
  64.7 5.9 %all-gather.6 = f32[4,16,128]{2,1,0:T(8,128)S(1)} all-gather(f32[2,16,128]{2,1,0:T(8,128)S(1)} %get-tuple-element.83), channel_id=8, replica_groups=mesh['row'=32,'pair'=12,'core'=2] {'core'}, dimensions={0}, use_global_device_ids=true | all-gather | bytes 49152 | tf_op jit(solution)/shard_map/all_gather | solution.py:59
  70.6 32.0 %conditional.3 = (f32[2,16,128]{2,1,0:T(8,128)S(1)}) conditional(s32[]{:T(128)} %convert_element_type.22, (bf16[2,16,128]{2,1,0:T(8,128)(2,1)S(1)}, s32[2]{0:T(128)S(1)}, f32[2,8]{1,0:T(2,128)S(1)}, s32[2,8]{1,0:T(2,128)S(1)}, s32[2,8]{1,0:T(2,128)S(1)}, /*index=5*/bf16[2,8,128,128]{3,2,1,0:T(8,128)(2,1)S(1)}) %tuple.39, ...), branch_computations={%region_5.0_spmd, %region_7.0_spmd} | conditional | flops 8646656 | bytes 1630216 | solution.py:89
  70.7 19.6 %all_to_all.36 = bf16[32,2,16,128]{3,2,1,0:T(8,128)(2,1)} all-to-all(bf16[32,2,16,128]{3,2,1,0:T(8,128)(2,1)S(1)} %broadcast_in_dim.17), channel_id=1, replica_groups=mesh['row'=32,'pair'=12,'core'=2] {'row'}, dimensions={0} | all-to-all | bytes 524288 | tf_op jit(solution)/shard_map/cond/branch_0_fun/all_to_all | solution.py:68
  90.3 2.0 %direct.3 = bf16[24,16,128]{2,1,0:T(8,128)(2,1)} custom-call(s32[2]{0:T(128)S(1)} %get-tuple-element.71.count_ref, f32[2,8]{1,0:T(2,128)S(1)} %get-tuple-element.72.scale_ref, s32[2,8]{1,0:T(2,128)S(1)} %get-tuple-element.73.row_ref, s32[2,8]{1,0:T(2,128)S(1)} %get-tuple-element.74.col_ref, bf16[64,16,128]{2,1,0:T(8,128)(2,1)} %bitcast.28, ...), custom_call_target="tpu_custom_call" | custom-call | flops 8388608 | bytes 524288 | tf_op jit(solution)/shard_map/cond/branch_0_fun/direct/pallas_call | solution.py:36
  92.3 10.3 %all_to_all.37 = bf16[12,2,16,128]{3,2,1,0:T(8,128)(2,1)S(1)} all-to-all(bf16[12,2,16,128]{3,2,1,0:T(8,128)(2,1)} %bitcast.32), channel_id=1, replica_groups=mesh['row'=32,'pair'=12,'core'=2] {'pair'}, dimensions={0} | all-to-all | bytes 196608 | tf_op jit(solution)/shard_map/cond/branch_0_fun/all_to_all | solution.py:68
  102.7 5.5 %all-gather.7 = f32[4,16,128]{2,1,0:T(8,128)S(1)} all-gather(f32[2,16,128]{2,1,0:T(8,128)S(1)} %get-tuple-element.84), channel_id=9, replica_groups=mesh['row'=32,'pair'=12,'core'=2] {'core'}, dimensions={0}, use_global_device_ids=true | all-gather | bytes 49152 | tf_op jit(solution)/shard_map/all_gather | solution.py:59
  108.1 0.6 fusion.2
  (12 shorter events, 0.1 us)
Async XLA Ops:
  2.0 12.7 %copy-start.1 = (f32[1,1,8]{2,1,0:T(1,128)S(1)}, f32[1,1,8]{2,1,0:T(1,128)}, u32[]{:S(2)}) copy-start(f32[1,1,8]{2,1,0:T(1,128)} %param.12) | copy-start | bytes 100
  2.0 14.5 %copy-start.2 = (s32[1,1,8]{2,1,0:T(1,128)S(1)}, s32[1,1,8]{2,1,0:T(1,128)}, u32[]{:S(2)}) copy-start(s32[1,1,8]{2,1,0:T(1,128)} %param.13) | copy-start | bytes 100
  2.0 18.8 %copy-start = (f32[16,128]{1,0:T(8,128)S(1)}, f32[16,128]{1,0:T(8,128)}, u32[]{:S(2)}) copy-start(f32[16,128]{1,0:T(8,128)} %param.10) | copy-start | bytes 24580
  18.3 0.7 copy-start.3

commit v3 on v2

v3 whole, which is shorter than its diff:
```python
import functools
import math

import jax
import jax.numpy as jnp
from jax import lax
from jax.experimental import pallas as pl
from jax.experimental.pallas import tpu as pltpu
from jax.sharding import Mesh
from jax.sharding import PartitionSpec as P

VMEM_LIMIT = 8 << 20
SMEM_BLOCK = pl.BlockSpec(memory_space=pltpu.SMEM)
VMEM_BLOCK = pl.BlockSpec(memory_space=pltpu.VMEM)


def pack_kernel(count_ref, start_ref, row_ref, col_ref, scale_ref, out_ref):
    vec_count, slots = start_ref.shape[0], row_ref.shape[1]
    out_ref[:vec_count] = start_ref[...]
    out_ref[vec_count:] = jnp.zeros_like(out_ref[vec_count:])
    slot = lax.broadcasted_iota(jnp.int32, (1, slots), 1)
    out_ref[vec_count : vec_count + 1, :slots] = row_ref[...].astype(jnp.float32)
    out_ref[vec_count + 1 : vec_count + 2, :slots] = col_ref[...].astype(jnp.float32)
    out_ref[vec_count + 2 : vec_count + 3, :slots] = jnp.where(slot < count_ref[0], scale_ref[...], 0.0)


def pack(start, rows, cols, scales, count):
    vec_count, width = start.shape
    return pl.pallas_call(
        pack_kernel,
        out_shape=jax.ShapeDtypeStruct((vec_count + 8, width), jnp.float32),
        in_specs=[SMEM_BLOCK, VMEM_BLOCK, VMEM_BLOCK, VMEM_BLOCK, VMEM_BLOCK],
        out_specs=VMEM_BLOCK,
        compiler_params=pltpu.CompilerParams(vmem_limit_bytes=VMEM_LIMIT),
        name="pack",
    )(count, start, rows, cols, scales)


def product_kernel(flipped, row_shift, row_size, pair_shift, pair_size, packed_ref, blocks_ref, tiles_ref, out_ref, acc_ref):
    acc_ref[...] = jnp.zeros_like(acc_ref)
    cores, slots = tiles_ref.shape[:2]
    stride = packed_ref.shape[0] // cores
    for core in range(cores):
        base = core * stride + blocks_ref.shape[1]
        for slot in range(slots):
            row = packed_ref[base, slot].astype(jnp.int32)
            col = packed_ref[base + 1, slot].astype(jnp.int32)
            weight = packed_ref[base + 2, slot]
            row = lax.rem(row + pair_shift * cores, pair_size * cores)
            col = lax.rem(col + row_shift, row_size) * cores + core
            source, target, contracted = (row, col, 0) if flipped else (col, row, 1)
            product = lax.dot_general(
                blocks_ref[source],
                tiles_ref[core, slot],
                (((1,), (contracted,)), ((), ())),
                preferred_element_type=jnp.float32,
            )
            acc_ref[target] = acc_ref[target] + product * weight
    out_ref[...] = acc_ref[...].astype(out_ref.dtype)


def body(row_lead, pair_lead, start_vectors, tile_values, tile_scales, tile_rows, tile_cols, tile_counts):
    total, tile_width = tile_values.shape[2:4]
    vec_count = start_vectors.shape[0]
    factor = 0.5 / math.sqrt(2.0 * total * tile_width)
    size = {axis: lax.axis_size(axis) for axis in ("row", "pair")}
    cores = lax.axis_size("core")
    lead = {"row": row_lead, "pair": pair_lead}
    shift = {axis: size[axis] - lead[axis] for axis in size}
    core = lax.axis_index("core")

    def both_cores(array):
        return lax.all_gather(array, "core", axis=0, tiled=True)

    packed = both_cores(pack(start_vectors, tile_rows[0], tile_cols[0], tile_scales[0], tile_counts[0]))
    tile_vals = both_cores(tile_values[0])

    def exchange(blocks, axis):
        order = [(lead[axis] + i) % size[axis] for i in range(size[axis])]
        return lax.all_to_all(blocks, axis, 0, 0, tiled=True, axis_index_groups=[order])

    def products(blocks, groups, flipped):
        kernel = functools.partial(
            product_kernel, flipped, shift["row"], size["row"], shift["pair"], size["pair"]
        )
        return pl.pallas_call(
            kernel,
            out_shape=jax.ShapeDtypeStruct((groups, vec_count, tile_width), jnp.bfloat16),
            in_specs=[SMEM_BLOCK, VMEM_BLOCK, VMEM_BLOCK],
            out_specs=VMEM_BLOCK,
            scratch_shapes=[pltpu.VMEM((groups, vec_count, tile_width), jnp.float32)],
            compiler_params=pltpu.CompilerParams(vmem_limit_bytes=VMEM_LIMIT),
            name="flipped" if flipped else "direct",
        )(packed, blocks, tile_vals)

    def chain(out_axis, back_axis, flipped, make_blocks, operand):
        blocks = make_blocks(operand).astype(jnp.bfloat16)
        got = exchange(jnp.broadcast_to(blocks[None], (size[out_axis], *blocks.shape)), out_axis)
        got = got.reshape(size[out_axis] * cores, vec_count, tile_width)
        partial = products(got, size[back_axis] * cores, flipped)
        parts = exchange(partial.reshape(size[back_axis], cores, vec_count, tile_width), back_axis)
        return jnp.sum(parts, axis=0, dtype=jnp.float32)

    def operate(make_blocks, operand):
        mine = lax.cond(
            core == 0,
            functools.partial(chain, "pair", "row", True, make_blocks),
            functools.partial(chain, "row", "pair", False, make_blocks),
            operand,
        )
        return both_cores(mine).reshape(2, cores, vec_count, tile_width)

    def start_blocks(array):
        return array.reshape(cores, -1, tile_width)[:, :vec_count]

    def next_blocks(parts):
        return factor * (parts[0] + parts[1])

    parts = operate(start_blocks, packed)
    parts = operate(next_blocks, parts)
    mine = lax.dynamic_index_in_dim(parts, core, 1, keepdims=False)
    return 2.0 * factor * (mine[0] + mine[1]) - start_vectors


def solution(mesh):
    rows, cols = mesh.devices.shape
    pairs = cols // 2
    split = Mesh(mesh.devices.reshape(rows, pairs, 2), ("row", "pair", "core"))
    columns = ("pair", "core")
    in_specs = (
        P(None, (*columns, "row")),
        P("row", columns, None, None, None),
        P("row", columns, None),
        P("row", columns, None),
        P("row", columns, None),
        P("row", columns),
    )
    out_specs = P(None, (*columns, "row"))
    step = functools.partial(body, rows * 5 // 8, pairs // 3)
    return jax.shard_map(step, mesh=split, in_specs=in_specs, out_specs=out_specs, check_vma=False)
```

time: 109 us -> 91.8 us (0.84)
  blocking collectives: 101 us -> 86.6 us
  local copies, waits for them, and re-layouts: 2.84 us -> 0.74 us
  Pallas kernels: 4.01 us -> 2.68 us
    all_to_all x4, blocking collectives: 67.6 us -> 59 us  [exchange(): lax.all_to_all(blocks, axis, 0, 0, tiled=True, axis_index_groups=[order])]
    all_gather x8 -> x4, blocking collectives: 33 us -> 27.7 us  [both_cores(): return lax.all_gather(array, 'core', axis=0, tiled=True)]
    unnamed x11 -> x8, local copies, waits for them, and re-layouts: 2.77 us -> 0.66 us
    pallas_call x2 -> x3, Pallas kernels: 4.01 us -> 2.68 us  [the longest x2 2.67 us: products(): pl.pallas_call(kernel, out_shape=jax.ShapeDtypeStruct((groups, vec_count,...]
where the time goes in v3:
time: 91.8 us; the launch traced here: 91.5 us
  blocking collectives  86.6 us (94%)
  Pallas kernels  2.68 us (3%)
    all_to_all x4, blocking collectives, exchange(): lax.all_to_all(blocks, axis, 0, 0, tiled=True, axis_index_groups=[order])  59 us
    all_gather x4, blocking collectives, both_cores(): return lax.all_gather(array, 'core', axis=0, tiled=True)  27.7 us
    pallas_call x2, Pallas kernels, products(): pl.pallas_call(kernel, out_shape=jax.ShapeDtypeStruct((groups, vec_count,...  2.67 us

profile of v3, /device:TPU:1, one launch (start us, length us, event | category | flops | bytes accessed | tf_op | source)
XLA Modules:
  0.0 91.5 jit_solution(5658336818705059569)
XLA Ops:
  0.0 12.5 %all-gather = bf16[2,1,8,128,128]{4,3,2,1,0:T(8,128)(2,1)S(1)} all-gather(bf16[1,1,8,128,128]{4,3,2,1,0:T(8,128)(2,1)} %param.11), channel_id=2, replica_groups=mesh['row'=32,'pair'=12,'core'=2] {'core'}, dimensions={0}, use_global_device_ids=true | all-gather | bytes 786432 | tf_op jit(solution)/shard_map/all_gather | solution.py:73
  12.5 0.0 copy-start
  13.2 0.0 copy-start.1
  13.2 0.0 copy-start.2
  13.2 0.0 copy-start.3
  13.2 0.0 copy-done
  13.2 0.6 copy-done.1
  13.8 0.0 copy-done.2
  13.8 0.0 copy-done.3
  13.8 1.8 %all_gather.12 = f32[48,128]{1,0:T(8,128)S(1)} all-gather(f32[24,128]{1,0:T(8,128)S(1)} %pack.1), channel_id=1, replica_groups=mesh['row'=32,'pair'=12,'core'=2] {'core'}, dimensions={0}, use_global_device_ids=true | all-gather | bytes 36864 | tf_op jit(solution)/shard_map/all_gather | solution.py:73
  15.7 31.2 %conditional.2 = (f32[2,16,128]{2,1,0:T(8,128)S(1)}) conditional(s32[]{:T(128)} %convert_element_type.26, (f32[48,128]{1,0:T(8,128)S(1)}, bf16[2,8,128,128]{3,2,1,0:T(8,128)(2,1)S(1)}) %tuple.23, (f32[48,128]{1,0:T(8,128)S(1)}, bf16[2,8,128,128]{3,2,1,0:T(8,128)(2,1)S(1)}) %tuple.24), branch_computations={%region_0.0_spmd, %region_2.0_spmd} | conditional | flops 264192 | bytes 1159176 | solution.py:105
  15.7 19.4 %all_to_all.32 = bf16[32,2,16,128]{3,2,1,0:T(8,128)(2,1)S(1)} all-to-all(bf16[32,2,16,128]{3,2,1,0:T(8,128)(2,1)S(1)} %broadcast_in_dim.8), channel_id=1, replica_groups={{480,504,528,552,576,600,624,648,672,696,720,744,0,24,48,72,96,120,144,..., dimensions={0} | all-to-all | bytes 524288 | tf_op jit(solution)/shard_map/cond/branch_0_fun/all_to_all | solution.py:80
  35.1 1.3 %direct.2 = bf16[24,16,128]{2,1,0:T(8,128)(2,1)S(1)} custom-call(f32[48,128]{1,0:T(8,128)S(1)} %get-tuple-element.30.packed_ref, bf16[64,16,128]{2,1,0:T(8,128)(2,1)S(1)} %bitcast.26, bf16[2,8,128,128]{3,2,1,0:T(8,128)(2,1)S(1)} %get-tuple-element.32.tiles_ref), custom_call_target="tpu_custom_call" | custom-call | tf_op jit(solution)/shard_map/cond/branch_0_fun/direct/pallas_call | solution.py:86
  36.5 10.4 %all_to_all.33 = bf16[12,2,16,128]{3,2,1,0:T(8,128)(2,1)S(1)} all-to-all(bf16[12,2,16,128]{3,2,1,0:T(8,128)(2,1)S(1)} %bitcast.30), channel_id=1, replica_groups={{8,10,12,14,16,18,20,22,0,2,4,6},{9,11,13,15,17,19,21,23,1,3,5,7},{32,3..., dimensions={0} | all-to-all | bytes 196608 | tf_op jit(solution)/shard_map/cond/branch_0_fun/all_to_all | solution.py:80
  46.9 6.2 %all_gather.14 = f32[4,16,128]{2,1,0:T(8,128)S(1)} all-gather(f32[2,16,128]{2,1,0:T(8,128)S(1)} %get-tuple-element.41), channel_id=1, replica_groups=mesh['row'=32,'pair'=12,'core'=2] {'core'}, dimensions={0}, use_global_device_ids=true | all-gather | bytes 49152 | tf_op jit(solution)/shard_map/all_gather | solution.py:73
  53.1 30.6 %conditional.3 = (f32[2,16,128]{2,1,0:T(8,128)S(1)}) conditional(s32[]{:T(128)} %convert_element_type.26, (f32[2,2,16,128]{3,2,1,0:T(8,128)S(1)}, f32[48,128]{1,0:T(8,128)S(1)}, bf16[2,8,128,128]{3,2,1,0:T(8,128)(2,1)S(1)}) %tuple.27, (f32[2,2,16,128]{3,2,1,0:T(8,128)S(1)}, f32[48,128]{1,0:T(8,128)S(1)}, bf16[2,8,128,128]{3,2,1,0:T(8,128)(2,1)S(1)}) %tuple.28), branch_computations={%region_4.0_spmd, %region_6.0_spmd} | conditional | flops 270336 | bytes 1146888 | solution.py:105
  53.1 18.0 %all_to_all.36 = bf16[32,2,16,128]{3,2,1,0:T(8,128)(2,1)S(1)} all-to-all(bf16[32,2,16,128]{3,2,1,0:T(8,128)(2,1)S(1)} %broadcast_in_dim.17), channel_id=1, replica_groups={{480,504,528,552,576,600,624,648,672,696,720,744,0,24,48,72,96,120,144,..., dimensions={0} | all-to-all | bytes 524288 | tf_op jit(solution)/shard_map/cond/branch_0_fun/all_to_all | solution.py:80
  71.2 1.3 %direct.3 = bf16[24,16,128]{2,1,0:T(8,128)(2,1)S(1)} custom-call(f32[48,128]{1,0:T(8,128)S(1)} %get-tuple-element.35.packed_ref, bf16[64,16,128]{2,1,0:T(8,128)(2,1)S(1)} %bitcast.28, bf16[2,8,128,128]{3,2,1,0:T(8,128)(2,1)S(1)} %get-tuple-element.37.tiles_ref), custom_call_target="tpu_custom_call" | custom-call | tf_op jit(solution)/shard_map/cond/branch_0_fun/direct/pallas_call | solution.py:86
  72.5 11.2 %all_to_all.37 = bf16[12,2,16,128]{3,2,1,0:T(8,128)(2,1)S(1)} all-to-all(bf16[12,2,16,128]{3,2,1,0:T(8,128)(2,1)S(1)} %bitcast.32), channel_id=1, replica_groups={{8,10,12,14,16,18,20,22,0,2,4,6},{9,11,13,15,17,19,21,23,1,3,5,7},{32,3..., dimensions={0} | all-to-all | bytes 196608 | tf_op jit(solution)/shard_map/cond/branch_0_fun/all_to_all | solution.py:80
  83.7 7.1 %all_gather.15 = f32[4,16,128]{2,1,0:T(8,128)S(1)} all-gather(f32[2,16,128]{2,1,0:T(8,128)S(1)} %get-tuple-element.42), channel_id=1, replica_groups=mesh['row'=32,'pair'=12,'core'=2] {'core'}, dimensions={0}, use_global_device_ids=true | all-gather | bytes 49152 | tf_op jit(solution)/shard_map/all_gather | solution.py:73
  90.9 0.6 fusion.4
  (8 shorter events, 0.1 us)
Async XLA Ops:
  12.5 0.7 copy-start
  13.2 0.7 copy-start.1
  13.2 0.7 copy-start.2
  13.2 0.7 copy-start.3

commit v4 on v3

v4 whole, which is shorter than its diff:
```python
import functools
import math

import jax
import jax.numpy as jnp
from jax import lax
from jax.experimental import pallas as pl
from jax.experimental.pallas import tpu as pltpu
from jax.sharding import Mesh
from jax.sharding import PartitionSpec as P

VMEM_LIMIT = 8 << 20
PACK_LIMIT = 60 << 20
META = 16
LEADS = (4, 20, 18, 4)
SMEM_BLOCK = pl.BlockSpec(memory_space=pltpu.SMEM)
VMEM_BLOCK = pl.BlockSpec(memory_space=pltpu.VMEM)
HBM_BLOCK = pl.BlockSpec(memory_space=pltpu.HBM)


def pack_kernel(count_in, start_in, row_in, col_in, scale_in, tile_in, out_ref, count, start, row, col, scale, sems):
    vec_count, slots = start_in.shape[0], row_in.shape[-1]
    pairs = (
        (count_in, count),
        (start_in, start),
        (row_in, row),
        (col_in, col),
        (scale_in, scale),
        (tile_in, out_ref.at[pl.ds(vec_count + META, tile_in.shape[0])]),
    )
    copies = [pltpu.make_async_copy(source, target, sems.at[i]) for i, (source, target) in enumerate(pairs)]
    for copy in copies:
        copy.start()
    for copy in copies[:-1]:
        copy.wait()
    slot = lax.broadcasted_iota(jnp.int32, (1, slots), 1)
    weight = jnp.where(slot < count[0, 0], scale[...], 0.0)
    high = weight.astype(jnp.bfloat16).astype(jnp.float32)
    middle = (weight - high).astype(jnp.bfloat16).astype(jnp.float32)
    low = weight - high - middle
    lines = [row[...].astype(jnp.float32), col[...].astype(jnp.float32), high, middle, low]
    lines = jnp.concatenate([*lines, jnp.zeros((META - len(lines), slots), jnp.float32)], axis=0)
    out_ref[:vec_count] = start[...].astype(jnp.bfloat16)
    out_ref[vec_count : vec_count + META] = jnp.zeros((META, out_ref.shape[1]), jnp.bfloat16)
    out_ref[vec_count : vec_count + META, :slots] = lines.astype(jnp.bfloat16)
    copies[-1].wait()


def pack(start, rows, cols, scales, count, tiles):
    vec_count, width = start.shape
    slots = tiles.shape[0]
    return pl.pallas_call(
        pack_kernel,
        out_shape=jax.ShapeDtypeStruct((vec_count + META + slots * width, width), jnp.bfloat16),
        in_specs=[HBM_BLOCK] * 6,
        out_specs=VMEM_BLOCK,
        scratch_shapes=[
            pltpu.SMEM((1, 1), jnp.int32),
            pltpu.VMEM((vec_count, width), jnp.float32),
            pltpu.VMEM((1, slots), jnp.int32),
            pltpu.VMEM((1, slots), jnp.int32),
            pltpu.VMEM((1, slots), jnp.float32),
            pltpu.SemaphoreType.DMA((6,)),
        ],
        compiler_params=pltpu.CompilerParams(vmem_limit_bytes=PACK_LIMIT),
        name="pack",
    )(count, start, rows, cols, scales, tiles.reshape(slots * width, width))


def unpack_kernel(shifts, packed_ref, start_ref, place_ref, weight_ref, kept_ref):
    cores, vec_count = packed_ref.shape[0], start_ref.shape[0]
    kept_ref[...] = start_ref[...]
    for core in range(cores):
        lines = packed_ref[core, vec_count : vec_count + META].astype(jnp.float32)
        row = lines[0:1].astype(jnp.int32)
        col = lines[1:2].astype(jnp.int32) * cores + core
        for i, (index, (shift, size)) in enumerate(zip((row, col, col, row), shifts)):
            place = index + shift * cores
            line = len(shifts) * core + i
            place_ref[line : line + 1] = jnp.where(place >= size * cores, place - size * cores, place)
        weight_ref[core : core + 1] = lines[2:3] + lines[3:4] + lines[4:5]


def product_kernel(flipped, slots, place_ref, weight_ref, packed_ref, blocks_ref, out_ref, acc_ref):
    acc_ref[...] = jnp.zeros_like(acc_ref)
    cores, _, width = packed_ref.shape
    first = blocks_ref.shape[1] + META
    for core in range(cores):
        for slot in range(slots):
            line = 4 * core + (0 if flipped else 2)
            source = place_ref[line, slot]
            target = place_ref[line + 1, slot]
            product = lax.dot_general(
                blocks_ref[source],
                packed_ref[core, first + slot * width : first + (slot + 1) * width],
                (((1,), (0 if flipped else 1,)), ((), ())),
                preferred_element_type=jnp.float32,
            )
            acc_ref[target] = acc_ref[target] + product * weight_ref[core, slot]
    out_ref[...] = acc_ref[...].astype(out_ref.dtype)


def body(leads, start_vectors, tile_values, tile_scales, tile_rows, tile_cols, tile_counts):
    total, tile_width = tile_values.shape[2:4]
    vec_count = start_vectors.shape[0]
    factor = 0.5 / math.sqrt(2.0 * total * tile_width)
    size = {axis: lax.axis_size(axis) for axis in ("row", "pair")}
    cores = lax.axis_size("core")
    axes = ("pair", "row", "row", "pair")
    shifts = tuple((size[axis] - lead, size[axis]) for axis, lead in zip(axes, leads))
    core = lax.axis_index("core")

    def both_cores(array):
        return lax.all_gather(array, "core", axis=0, tiled=True)

    packed = both_cores(
        pack(start_vectors, tile_rows[0], tile_cols[0], tile_scales[0], tile_counts, tile_values[0, 0])[None]
    )
    place, weight, kept = pl.pallas_call(
        functools.partial(unpack_kernel, shifts),
        out_shape=(
            jax.ShapeDtypeStruct((len(axes) * cores, tile_width), jnp.int32),
            jax.ShapeDtypeStruct((cores, tile_width), jnp.float32),
            jax.ShapeDtypeStruct(start_vectors.shape, jnp.float32),
        ),
        in_specs=[VMEM_BLOCK, VMEM_BLOCK],
        out_specs=(VMEM_BLOCK, VMEM_BLOCK, VMEM_BLOCK),
        compiler_params=pltpu.CompilerParams(vmem_limit_bytes=VMEM_LIMIT),
        name="unpack",
    )(packed, start_vectors)

    def exchange(blocks, leg):
        axis, lead = axes[leg], leads[leg]
        order = [(lead + i) % size[axis] for i in range(size[axis])]
        return lax.all_to_all(blocks, axis, 0, 0, tiled=True, axis_index_groups=[order])

    def products(blocks, groups, flipped):
        return pl.pallas_call(
            functools.partial(product_kernel, flipped, total),
            out_shape=jax.ShapeDtypeStruct((groups, vec_count, tile_width), jnp.bfloat16),
            in_specs=[SMEM_BLOCK, SMEM_BLOCK, VMEM_BLOCK, VMEM_BLOCK],
            out_specs=VMEM_BLOCK,
            scratch_shapes=[pltpu.VMEM((groups, vec_count, tile_width), jnp.float32)],
            compiler_params=pltpu.CompilerParams(vmem_limit_bytes=VMEM_LIMIT),
            name="flipped" if flipped else "direct",
        )(place, weight, packed, blocks)

    def chain(leg, make_blocks, operand):
        out_size, back_size = size[axes[leg]], size[axes[leg + 1]]
        blocks = make_blocks(operand).astype(jnp.bfloat16)
        got = exchange(jnp.broadcast_to(blocks[None], (out_size, *blocks.shape)), leg)
        partial = products(got.reshape(out_size * cores, vec_count, tile_width), back_size * cores, leg == 0)
        parts = exchange(partial.reshape(back_size, cores, vec_count, tile_width), leg + 1)
        return jnp.sum(parts, axis=0, dtype=jnp.float32)

    def operate(make_blocks, operand):
        mine = lax.cond(
            core == 0,
            functools.partial(chain, 0, make_blocks),
            functools.partial(chain, 2, make_blocks),
            operand,
        )
        return both_cores(mine).reshape(2, cores, vec_count, tile_width)

    def start_blocks(array):
        return array[:, :vec_count]

    def next_blocks(parts):
        return factor * (parts[0] + parts[1])

    parts = operate(start_blocks, packed)
    parts = operate(next_blocks, parts)
    mine = lax.dynamic_index_in_dim(parts, core, 1, keepdims=False)
    return 2.0 * factor * (mine[0] + mine[1]) - kept


def solution(mesh):
    rows, cols = mesh.devices.shape
    pairs = cols // 2
    split = Mesh(mesh.devices.reshape(rows, pairs, 2), ("row", "pair", "core"))
    columns = ("pair", "core")
    in_specs = (
        P(None, (*columns, "row")),
        P("row", columns, None, None, None),
        P("row", columns, None),
        P("row", columns, None),
        P("row", columns, None),
        P("row", columns),
    )
    out_specs = P(None, (*columns, "row"))
    step = functools.partial(body, LEADS)
    return jax.shard_map(step, mesh=split, in_specs=in_specs, out_specs=out_specs, check_vma=False)
```

time: 91.8 us -> 87.4 us (0.952)
  blocking collectives: 86.6 us -> 81.8 us
  Pallas kernels: 2.68 us -> 3.8 us
    all_gather x4 -> x3, blocking collectives: 27.7 us -> 16.2 us  [both_cores(): return lax.all_gather(array, 'core', axis=0, tiled=True)]
    all_to_all x4, blocking collectives: 59 us -> 65.6 us  [exchange(): lax.all_to_all(blocks, axis, 0, 0, tiled=True, axis_index_groups=[order])]
    pallas_call x3 -> x4, Pallas kernels: 2.68 us -> 3.8 us  [the longest x2 2.02 us: products(): pl.pallas_call(functools.partial(product_kernel, flipped, total), out_sha...]
where the time goes in v4:
time: 87.4 us; the launch traced here: 87.1 us
  blocking collectives  81.8 us (94%)
  Pallas kernels  3.8 us (4%)
    all_to_all x4, blocking collectives, exchange(): lax.all_to_all(blocks, axis, 0, 0, tiled=True, axis_index_groups=[order])  65.6 us
    all_gather x3, blocking collectives, both_cores(): return lax.all_gather(array, 'core', axis=0, tiled=True)  16.2 us
    pallas_call x2, Pallas kernels, products(): pl.pallas_call(functools.partial(product_kernel, flipped, total), out_sha...  2.02 us
    pallas_call x1, Pallas kernels, pack(): pl.pallas_call(pack_kernel, out_shape=jax.ShapeDtypeStruct((vec_count + M...  1.77 us

profile of v4, /device:TPU:1, one launch (start us, length us, event | category | flops | bytes accessed | tf_op | source)
XLA Modules:
  0.0 87.1 jit_solution(12585084801162458207)
XLA Ops:
  0.7 1.8 %pack.1 = bf16[1056,128]{1,0:T(8,128)(2,1)} custom-call(s32[1,1]{1,0:T(1,128)S(6)} %copy.11.count_in, f32[16,128]{1,0:T(8,128)} %start_ref.1, s32[1,8]{1,0:T(1,128)} %bitcast.40, s32[1,8]{1,0:T(1,128)} %bitcast.41, f32[1,8]{1,0:T(1,128)} %bitcast.42, bf16[1024,128]{1,0:T(8,128)(2,1)} %bitcast.38), custom_call_target="tpu_custom_call" | custom-call | tf_op jit(solution)/shard_map/pack/pallas_call | solution.py:52
  2.4 0.0 copy-start
  2.4 12.5 %all-gather = bf16[2112,128]{1,0:T(8,128)(2,1)S(1)} all-gather(bf16[1056,128]{1,0:T(8,128)(2,1)} %pack.1), channel_id=2, replica_groups=mesh['row'=32,'pair'=12,'core'=2] {'core'}, dimensions={0}, use_global_device_ids=true | all-gather | bytes 811008 | tf_op jit(solution)/shard_map/all_gather | solution.py:114
  15.0 0.0 copy-done
  15.0 35.1 %conditional.2 = (f32[2,16,128]{2,1,0:T(8,128)S(1)}) conditional(s32[]{:T(128)} %convert_element_type.24, (bf16[2,1056,128]{2,1,0:T(8,128)(2,1)S(1)}, s32[8,128]{1,0:T(8,128)S(1)}, f32[2,128]{1,0:T(2,128)S(1)}) %tuple.23, (bf16[2,1056,128]{2,1,0:T(8,128)(2,1)S(1)}, s32[8,128]{1,0:T(8,128)S(1)}, f32[2,128]{1,0:T(2,128)S(1)}) %tuple.24), branch_computations={%region_0.0_spmd, %region_2.0_spmd} | conditional | flops 258048 | bytes 1122312 | solution.py:157
  15.0 22.1 %all_to_all.32 = bf16[32,2,16,128]{3,2,1,0:T(8,128)(2,1)S(1)} all-to-all(bf16[32,2,16,128]{3,2,1,0:T(8,128)(2,1)S(1)} %broadcast_in_dim.9), channel_id=1, replica_groups={{432,456,480,504,528,552,576,600,624,648,672,696,720,744,0,24,48,72,96,..., dimensions={0} | all-to-all | bytes 524288 | tf_op jit(solution)/shard_map/cond/branch_0_fun/all_to_all | solution.py:135
  37.1 1.0 %direct.2 = bf16[24,16,128]{2,1,0:T(8,128)(2,1)S(1)} custom-call(s32[8,128]{1,0:T(8,128)S(1)} %get-tuple-element.38.place_ref, f32[2,128]{1,0:T(2,128)S(1)} %get-tuple-element.40.weight_ref, bf16[2,1056,128]{2,1,0:T(8,128)(2,1)S(1)} %get-tuple-element.41.packed_ref, bf16[64,16,128]{2,1,0:T(8,128)(2,1)S(1)} %bitcast.23), custom_call_target="tpu_custom_call" | custom-call | tf_op jit(solution)/shard_map/cond/branch_0_fun/direct/pallas_call | solution.py:138
  38.1 11.9 %all_to_all.33 = bf16[12,2,16,128]{3,2,1,0:T(8,128)(2,1)S(1)} all-to-all(bf16[12,2,16,128]{3,2,1,0:T(8,128)(2,1)S(1)} %bitcast.27), channel_id=1, replica_groups={{8,10,12,14,16,18,20,22,0,2,4,6},{9,11,13,15,17,19,21,23,1,3,5,7},{32,3..., dimensions={0} | all-to-all | bytes 196608 | tf_op jit(solution)/shard_map/cond/branch_0_fun/all_to_all | solution.py:135
  50.0 1.8 %all_gather.10 = f32[4,16,128]{2,1,0:T(8,128)S(1)} all-gather(f32[2,16,128]{2,1,0:T(8,128)S(1)} %get-tuple-element.59), channel_id=1, replica_groups=mesh['row'=32,'pair'=12,'core'=2] {'core'}, dimensions={0}, use_global_device_ids=true | all-gather | bytes 49152 | tf_op jit(solution)/shard_map/all_gather | solution.py:114
  51.9 32.8 %conditional.3 = (f32[2,16,128]{2,1,0:T(8,128)S(1)}) conditional(s32[]{:T(128)} %convert_element_type.24, (f32[2,2,16,128]{3,2,1,0:T(8,128)S(1)}, s32[8,128]{1,0:T(8,128)S(1)}, f32[2,128]{1,0:T(2,128)S(1)}, bf16[2,1056,128]{2,1,0:T(8,128)(2,1)S(1)}) %tuple.27, (f32[2,2,16,128]{3,2,1,0:T(8,128)S(1)}, s32[8,128]{1,0:T(8,128)S(1)}, ...), branch_computations={%region_4.0_spmd, %region_6.0_spmd} | conditional | flops 270336 | bytes 1146888 | solution.py:157
  51.9 21.4 %all_to_all.36 = bf16[32,2,16,128]{3,2,1,0:T(8,128)(2,1)S(1)} all-to-all(bf16[32,2,16,128]{3,2,1,0:T(8,128)(2,1)S(1)} %broadcast_in_dim.18), channel_id=1, replica_groups={{432,456,480,504,528,552,576,600,624,648,672,696,720,744,0,24,48,72,96,..., dimensions={0} | all-to-all | bytes 524288 | tf_op jit(solution)/shard_map/cond/branch_0_fun/all_to_all | solution.py:135
  73.3 1.0 %direct.3 = bf16[24,16,128]{2,1,0:T(8,128)(2,1)S(1)} custom-call(s32[8,128]{1,0:T(8,128)S(1)} %get-tuple-element.45.place_ref, f32[2,128]{1,0:T(2,128)S(1)} %get-tuple-element.46.weight_ref, bf16[2,1056,128]{2,1,0:T(8,128)(2,1)S(1)} %get-tuple-element.47.packed_ref, bf16[64,16,128]{2,1,0:T(8,128)(2,1)S(1)} %bitcast.25), custom_call_target="tpu_custom_call" | custom-call | tf_op jit(solution)/shard_map/cond/branch_0_fun/direct/pallas_call | solution.py:138
  74.3 10.3 %all_to_all.37 = bf16[12,2,16,128]{3,2,1,0:T(8,128)(2,1)S(1)} all-to-all(bf16[12,2,16,128]{3,2,1,0:T(8,128)(2,1)S(1)} %bitcast.29), channel_id=1, replica_groups={{8,10,12,14,16,18,20,22,0,2,4,6},{9,11,13,15,17,19,21,23,1,3,5,7},{32,3..., dimensions={0} | all-to-all | bytes 196608 | tf_op jit(solution)/shard_map/cond/branch_0_fun/all_to_all | solution.py:135
  84.7 1.8 %all_gather.11 = f32[4,16,128]{2,1,0:T(8,128)S(1)} all-gather(f32[2,16,128]{2,1,0:T(8,128)S(1)} %get-tuple-element.60), channel_id=1, replica_groups=mesh['row'=32,'pair'=12,'core'=2] {'core'}, dimensions={0}, use_global_device_ids=true | all-gather | bytes 49152 | tf_op jit(solution)/shard_map/all_gather | solution.py:114
  86.5 0.6 fusion.4
  (7 shorter events, 0.1 us)
Async XLA Ops:
  2.4 12.5 %copy-start = (f32[16,128]{1,0:T(8,128)S(1)}, f32[16,128]{1,0:T(8,128)}, u32[]{:S(2)}) copy-start(f32[16,128]{1,0:T(8,128)} %start_ref.1) | copy-start | bytes 24580

commit v5 on v4

--- a/solution.py
+++ b/solution.py
@@ -10,7 +10,7 @@
 from jax.sharding import PartitionSpec as P
 
 VMEM_LIMIT = 8 << 20
-PACK_LIMIT = 60 << 20
+PACK_LIMIT = 8 << 20
 META = 16
 LEADS = (4, 20, 18, 4)
 SMEM_BLOCK = pl.BlockSpec(memory_space=pltpu.SMEM)
@@ -49,6 +49,8 @@
 def pack(start, rows, cols, scales, count, tiles):
     vec_count, width = start.shape
     slots = tiles.shape[0]
+    arrays = (start, rows, cols, scales, tiles.reshape(slots * width, width))
+    arrays = [pltpu.with_memory_space_constraint(array, pltpu.HBM) for array in arrays]
     return pl.pallas_call(
         pack_kernel,
         out_shape=jax.ShapeDtypeStruct((vec_count + META + slots * width, width), jnp.bfloat16),
@@ -64,7 +66,7 @@
         ],
         compiler_params=pltpu.CompilerParams(vmem_limit_bytes=PACK_LIMIT),
         name="pack",
-    )(count, start, rows, cols, scales, tiles.reshape(slots * width, width))
+    )(count, *arrays)
 
 
 def unpack_kernel(shifts, packed_ref, start_ref, place_ref, weight_ref, kept_ref):

time: 87.4 us -> 86.5 us (0.990)
  no operation moved by 1% of the time
where the time goes in v5:
time: 86.5 us; the launch traced here: 86.2 us
  blocking collectives  81.6 us (94%)
  Pallas kernels  3.1 us (4%)
    all_to_all x4, blocking collectives, exchange(): lax.all_to_all(blocks, axis, 0, 0, tiled=True, axis_index_groups=[order])  65.6 us
    all_gather x3, blocking collectives, both_cores(): return lax.all_gather(array, 'core', axis=0, tiled=True)  16 us
    pallas_call x2, Pallas kernels, products(): pl.pallas_call(functools.partial(product_kernel, flipped, total), out_sha...  2.02 us

profile of v5, /device:TPU:1, one launch (start us, length us, event | category | flops | bytes accessed | tf_op | source)
XLA Modules:
  0.0 86.2 jit_solution(1858114337487598403)
XLA Ops:
  0.7 1.1 %pack.1 = bf16[1056,128]{1,0:T(8,128)(2,1)S(1)} custom-call(s32[1,1]{1,0:T(1,128)S(6)} %copy.11.count_in, f32[16,128]{1,0:T(8,128)} %start_ref.1, s32[1,8]{1,0:T(1,128)} %bitcast.40, s32[1,8]{1,0:T(1,128)} %bitcast.41, f32[1,8]{1,0:T(1,128)} %bitcast.42, bf16[1024,128]{1,0:T(8,128)(2,1)} %bitcast.38), custom_call_target="tpu_custom_call" | custom-call | tf_op jit(solution)/shard_map/pack/pallas_call | solution.py:54
  1.7 0.0 copy-start
  1.7 12.3 %all-gather = bf16[2112,128]{1,0:T(8,128)(2,1)S(1)} all-gather(bf16[1056,128]{1,0:T(8,128)(2,1)S(1)} %pack.1), channel_id=2, replica_groups=mesh['row'=32,'pair'=12,'core'=2] {'core'}, dimensions={0}, use_global_device_ids=true | all-gather | bytes 811008 | tf_op jit(solution)/shard_map/all_gather | solution.py:116
  14.0 0.0 copy-done
  14.1 35.0 %conditional.2 = (f32[2,16,128]{2,1,0:T(8,128)S(1)}) conditional(s32[]{:T(128)} %convert_element_type.24, (bf16[2,1056,128]{2,1,0:T(8,128)(2,1)S(1)}, s32[8,128]{1,0:T(8,128)S(1)}, f32[2,128]{1,0:T(2,128)S(1)}) %tuple.23, (bf16[2,1056,128]{2,1,0:T(8,128)(2,1)S(1)}, s32[8,128]{1,0:T(8,128)S(1)}, f32[2,128]{1,0:T(2,128)S(1)}) %tuple.24), branch_computations={%region_0.0_spmd, %region_2.0_spmd} | conditional | flops 258048 | bytes 1122312 | solution.py:159
  14.1 22.1 %all_to_all.32 = bf16[32,2,16,128]{3,2,1,0:T(8,128)(2,1)S(1)} all-to-all(bf16[32,2,16,128]{3,2,1,0:T(8,128)(2,1)S(1)} %broadcast_in_dim.9), channel_id=1, replica_groups={{432,456,480,504,528,552,576,600,624,648,672,696,720,744,0,24,48,72,96,..., dimensions={0} | all-to-all | bytes 524288 | tf_op jit(solution)/shard_map/cond/branch_0_fun/all_to_all | solution.py:137
  36.2 1.0 %direct.2 = bf16[24,16,128]{2,1,0:T(8,128)(2,1)S(1)} custom-call(s32[8,128]{1,0:T(8,128)S(1)} %get-tuple-element.38.place_ref, f32[2,128]{1,0:T(2,128)S(1)} %get-tuple-element.40.weight_ref, bf16[2,1056,128]{2,1,0:T(8,128)(2,1)S(1)} %get-tuple-element.41.packed_ref, bf16[64,16,128]{2,1,0:T(8,128)(2,1)S(1)} %bitcast.23), custom_call_target="tpu_custom_call" | custom-call | tf_op jit(solution)/shard_map/cond/branch_0_fun/direct/pallas_call | solution.py:140
  37.2 11.9 %all_to_all.33 = bf16[12,2,16,128]{3,2,1,0:T(8,128)(2,1)S(1)} all-to-all(bf16[12,2,16,128]{3,2,1,0:T(8,128)(2,1)S(1)} %bitcast.27), channel_id=1, replica_groups={{8,10,12,14,16,18,20,22,0,2,4,6},{9,11,13,15,17,19,21,23,1,3,5,7},{32,3..., dimensions={0} | all-to-all | bytes 196608 | tf_op jit(solution)/shard_map/cond/branch_0_fun/all_to_all | solution.py:137
  49.1 1.8 %all_gather.10 = f32[4,16,128]{2,1,0:T(8,128)S(1)} all-gather(f32[2,16,128]{2,1,0:T(8,128)S(1)} %get-tuple-element.59), channel_id=1, replica_groups=mesh['row'=32,'pair'=12,'core'=2] {'core'}, dimensions={0}, use_global_device_ids=true | all-gather | bytes 49152 | tf_op jit(solution)/shard_map/all_gather | solution.py:116
  50.9 32.8 %conditional.3 = (f32[2,16,128]{2,1,0:T(8,128)S(1)}) conditional(s32[]{:T(128)} %convert_element_type.24, (f32[2,2,16,128]{3,2,1,0:T(8,128)S(1)}, s32[8,128]{1,0:T(8,128)S(1)}, f32[2,128]{1,0:T(2,128)S(1)}, bf16[2,1056,128]{2,1,0:T(8,128)(2,1)S(1)}) %tuple.27, (f32[2,2,16,128]{3,2,1,0:T(8,128)S(1)}, s32[8,128]{1,0:T(8,128)S(1)}, ...), branch_computations={%region_4.0_spmd, %region_6.0_spmd} | conditional | flops 270336 | bytes 1146888 | solution.py:159
  51.0 21.4 %all_to_all.36 = bf16[32,2,16,128]{3,2,1,0:T(8,128)(2,1)S(1)} all-to-all(bf16[32,2,16,128]{3,2,1,0:T(8,128)(2,1)S(1)} %broadcast_in_dim.18), channel_id=1, replica_groups={{432,456,480,504,528,552,576,600,624,648,672,696,720,744,0,24,48,72,96,..., dimensions={0} | all-to-all | bytes 524288 | tf_op jit(solution)/shard_map/cond/branch_0_fun/all_to_all | solution.py:137
  72.4 1.0 %direct.3 = bf16[24,16,128]{2,1,0:T(8,128)(2,1)S(1)} custom-call(s32[8,128]{1,0:T(8,128)S(1)} %get-tuple-element.45.place_ref, f32[2,128]{1,0:T(2,128)S(1)} %get-tuple-element.46.weight_ref, bf16[2,1056,128]{2,1,0:T(8,128)(2,1)S(1)} %get-tuple-element.47.packed_ref, bf16[64,16,128]{2,1,0:T(8,128)(2,1)S(1)} %bitcast.25), custom_call_target="tpu_custom_call" | custom-call | tf_op jit(solution)/shard_map/cond/branch_0_fun/direct/pallas_call | solution.py:140
  73.4 10.3 %all_to_all.37 = bf16[12,2,16,128]{3,2,1,0:T(8,128)(2,1)S(1)} all-to-all(bf16[12,2,16,128]{3,2,1,0:T(8,128)(2,1)S(1)} %bitcast.29), channel_id=1, replica_groups={{8,10,12,14,16,18,20,22,0,2,4,6},{9,11,13,15,17,19,21,23,1,3,5,7},{32,3..., dimensions={0} | all-to-all | bytes 196608 | tf_op jit(solution)/shard_map/cond/branch_0_fun/all_to_all | solution.py:137
  83.8 1.8 %all_gather.11 = f32[4,16,128]{2,1,0:T(8,128)S(1)} all-gather(f32[2,16,128]{2,1,0:T(8,128)S(1)} %get-tuple-element.60), channel_id=1, replica_groups=mesh['row'=32,'pair'=12,'core'=2] {'core'}, dimensions={0}, use_global_device_ids=true | all-gather | bytes 49152 | tf_op jit(solution)/shard_map/all_gather | solution.py:116
  85.6 0.6 fusion.4
  (7 shorter events, 0.1 us)
Async XLA Ops:
  1.7 12.3 %copy-start = (f32[16,128]{1,0:T(8,128)S(1)}, f32[16,128]{1,0:T(8,128)}, u32[]{:S(2)}) copy-start(f32[16,128]{1,0:T(8,128)} %start_ref.1) | copy-start | bytes 24580

commit v6 on v5

--- a/solution.py
+++ b/solution.py
@@ -12,7 +12,7 @@
 VMEM_LIMIT = 8 << 20
 PACK_LIMIT = 8 << 20
 META = 16
-LEADS = (4, 20, 18, 4)
+LEADS = (4, 20, 13, 4)
 SMEM_BLOCK = pl.BlockSpec(memory_space=pltpu.SMEM)
 VMEM_BLOCK = pl.BlockSpec(memory_space=pltpu.VMEM)
 HBM_BLOCK = pl.BlockSpec(memory_space=pltpu.HBM)

time: 86.5 us -> 86.9 us (level)
  no operation moved by 1% of the time
where the time goes in v6:
time: 86.9 us; the launch traced here: 86.6 us
  blocking collectives  82 us (94%)
  Pallas kernels  3.1 us (4%)
    all_to_all x4, blocking collectives, exchange(): lax.all_to_all(blocks, axis, 0, 0, tiled=True, axis_index_groups=[order])  65.5 us
    all_gather x3, blocking collectives, both_cores(): return lax.all_gather(array, 'core', axis=0, tiled=True)  16.5 us
    pallas_call x2, Pallas kernels, products(): pl.pallas_call(functools.partial(product_kernel, flipped, total), out_sha...  2.02 us

profile of v6, /device:TPU:1, one launch (start us, length us, event | category | flops | bytes accessed | tf_op | source)
XLA Modules:
  0.0 86.6 jit_solution(2742402004627569278)
XLA Ops:
  0.7 1.1 %pack.1 = bf16[1056,128]{1,0:T(8,128)(2,1)S(1)} custom-call(s32[1,1]{1,0:T(1,128)S(6)} %copy.11.count_in, f32[16,128]{1,0:T(8,128)} %start_ref.1, s32[1,8]{1,0:T(1,128)} %bitcast.40, s32[1,8]{1,0:T(1,128)} %bitcast.41, f32[1,8]{1,0:T(1,128)} %bitcast.42, bf16[1024,128]{1,0:T(8,128)(2,1)} %bitcast.38), custom_call_target="tpu_custom_call" | custom-call | tf_op jit(solution)/shard_map/pack/pallas_call | solution.py:54
  1.7 0.0 copy-start
  1.7 12.3 %all-gather = bf16[2112,128]{1,0:T(8,128)(2,1)S(1)} all-gather(bf16[1056,128]{1,0:T(8,128)(2,1)S(1)} %pack.1), channel_id=2, replica_groups=mesh['row'=32,'pair'=12,'core'=2] {'core'}, dimensions={0}, use_global_device_ids=true | all-gather | bytes 811008 | tf_op jit(solution)/shard_map/all_gather | solution.py:116
  14.0 0.0 copy-done
  14.1 35.8 %conditional.2 = (f32[2,16,128]{2,1,0:T(8,128)S(1)}) conditional(s32[]{:T(128)} %convert_element_type.24, (bf16[2,1056,128]{2,1,0:T(8,128)(2,1)S(1)}, s32[8,128]{1,0:T(8,128)S(1)}, f32[2,128]{1,0:T(2,128)S(1)}) %tuple.23, (bf16[2,1056,128]{2,1,0:T(8,128)(2,1)S(1)}, s32[8,128]{1,0:T(8,128)S(1)}, f32[2,128]{1,0:T(2,128)S(1)}) %tuple.24), branch_computations={%region_0.0_spmd, %region_2.0_spmd} | conditional | flops 258048 | bytes 1122312 | solution.py:159
  14.1 22.9 %all_to_all.32 = bf16[32,2,16,128]{3,2,1,0:T(8,128)(2,1)S(1)} all-to-all(bf16[32,2,16,128]{3,2,1,0:T(8,128)(2,1)S(1)} %broadcast_in_dim.9), channel_id=1, replica_groups={{312,336,360,384,408,432,456,480,504,528,552,576,600,624,648,672,696,72..., dimensions={0} | all-to-all | bytes 524288 | tf_op jit(solution)/shard_map/cond/branch_0_fun/all_to_all | solution.py:137
  37.0 1.0 %direct.2 = bf16[24,16,128]{2,1,0:T(8,128)(2,1)S(1)} custom-call(s32[8,128]{1,0:T(8,128)S(1)} %get-tuple-element.38.place_ref, f32[2,128]{1,0:T(2,128)S(1)} %get-tuple-element.40.weight_ref, bf16[2,1056,128]{2,1,0:T(8,128)(2,1)S(1)} %get-tuple-element.41.packed_ref, bf16[64,16,128]{2,1,0:T(8,128)(2,1)S(1)} %bitcast.23), custom_call_target="tpu_custom_call" | custom-call | tf_op jit(solution)/shard_map/cond/branch_0_fun/direct/pallas_call | solution.py:140
  38.0 11.9 %all_to_all.33 = bf16[12,2,16,128]{3,2,1,0:T(8,128)(2,1)S(1)} all-to-all(bf16[12,2,16,128]{3,2,1,0:T(8,128)(2,1)S(1)} %bitcast.27), channel_id=1, replica_groups={{8,10,12,14,16,18,20,22,0,2,4,6},{9,11,13,15,17,19,21,23,1,3,5,7},{32,3..., dimensions={0} | all-to-all | bytes 196608 | tf_op jit(solution)/shard_map/cond/branch_0_fun/all_to_all | solution.py:137
  49.9 1.8 %all_gather.10 = f32[4,16,128]{2,1,0:T(8,128)S(1)} all-gather(f32[2,16,128]{2,1,0:T(8,128)S(1)} %get-tuple-element.59), channel_id=1, replica_groups=mesh['row'=32,'pair'=12,'core'=2] {'core'}, dimensions={0}, use_global_device_ids=true | all-gather | bytes 49152 | tf_op jit(solution)/shard_map/all_gather | solution.py:116
  51.7 31.8 %conditional.3 = (f32[2,16,128]{2,1,0:T(8,128)S(1)}) conditional(s32[]{:T(128)} %convert_element_type.24, (f32[2,2,16,128]{3,2,1,0:T(8,128)S(1)}, s32[8,128]{1,0:T(8,128)S(1)}, f32[2,128]{1,0:T(2,128)S(1)}, bf16[2,1056,128]{2,1,0:T(8,128)(2,1)S(1)}) %tuple.27, (f32[2,2,16,128]{3,2,1,0:T(8,128)S(1)}, s32[8,128]{1,0:T(8,128)S(1)}, ...), branch_computations={%region_4.0_spmd, %region_6.0_spmd} | conditional | flops 270336 | bytes 1146888 | solution.py:159
  51.8 21.0 %all_to_all.36 = bf16[32,2,16,128]{3,2,1,0:T(8,128)(2,1)S(1)} all-to-all(bf16[32,2,16,128]{3,2,1,0:T(8,128)(2,1)S(1)} %broadcast_in_dim.18), channel_id=1, replica_groups={{312,336,360,384,408,432,456,480,504,528,552,576,600,624,648,672,696,72..., dimensions={0} | all-to-all | bytes 524288 | tf_op jit(solution)/shard_map/cond/branch_0_fun/all_to_all | solution.py:137
  72.8 1.0 %direct.3 = bf16[24,16,128]{2,1,0:T(8,128)(2,1)S(1)} custom-call(s32[8,128]{1,0:T(8,128)S(1)} %get-tuple-element.45.place_ref, f32[2,128]{1,0:T(2,128)S(1)} %get-tuple-element.46.weight_ref, bf16[2,1056,128]{2,1,0:T(8,128)(2,1)S(1)} %get-tuple-element.47.packed_ref, bf16[64,16,128]{2,1,0:T(8,128)(2,1)S(1)} %bitcast.25), custom_call_target="tpu_custom_call" | custom-call | tf_op jit(solution)/shard_map/cond/branch_0_fun/direct/pallas_call | solution.py:140
  73.8 9.7 %all_to_all.37 = bf16[12,2,16,128]{3,2,1,0:T(8,128)(2,1)S(1)} all-to-all(bf16[12,2,16,128]{3,2,1,0:T(8,128)(2,1)S(1)} %bitcast.29), channel_id=1, replica_groups={{8,10,12,14,16,18,20,22,0,2,4,6},{9,11,13,15,17,19,21,23,1,3,5,7},{32,3..., dimensions={0} | all-to-all | bytes 196608 | tf_op jit(solution)/shard_map/cond/branch_0_fun/all_to_all | solution.py:137
  83.6 2.4 %all_gather.11 = f32[4,16,128]{2,1,0:T(8,128)S(1)} all-gather(f32[2,16,128]{2,1,0:T(8,128)S(1)} %get-tuple-element.60), channel_id=1, replica_groups=mesh['row'=32,'pair'=12,'core'=2] {'core'}, dimensions={0}, use_global_device_ids=true | all-gather | bytes 49152 | tf_op jit(solution)/shard_map/all_gather | solution.py:116
  86.0 0.6 fusion.4
  (7 shorter events, 0.1 us)
Async XLA Ops:
  1.7 12.3 %copy-start = (f32[16,128]{1,0:T(8,128)S(1)}, f32[16,128]{1,0:T(8,128)}, u32[]{:S(2)}) copy-start(f32[16,128]{1,0:T(8,128)} %start_ref.1) | copy-start | bytes 24580
